TPU v7x, 32 devices: a whole 2x2x4 slice. The times are simulated.
32 devices in a mesh: gx: 4 (over x, core), gy: 8 (over z, y).
Axes of the slice: x: 2, y: 2, z: 4, core: 2. Of those that a mesh axis runs over, the one named last changes fastest.
Arguments:
- weights: float32 [2, 64, 8, 16, 512], P(None, None, 'gx', 'gy'), may hold values from -6 to 6
- interp: float32 [4, 4, 64, 64], replicated, may hold values from -0.375 to 0.375
- travel: float32 [64, 4096], replicated, may hold values from -3.140625 to 3.140625
- entry_rows: int32 [3, 4, 8, 2048], P(None, 'gx', 'gy'), may hold values from 0 to 4095
- exit_rows: int32 [3, 4, 8, 2048], P(None, 'gx', 'gy'), may hold values from 0 to 4095
Outputs:
- result: float32 [2, 64, 1, 2, 32768], P(None, None, None, None, ('gx', 'gy'))
All inputs are finite; a program needn't handle non-finite values.
Results may differ from a plain program's by a relative error of at most 0.0001.
Values sent between devices are 32-bit elements; how exact they have to be, the bound alone decides.
A program may use at most 128 MiB of HBM per device.

v0:
```python
import functools

import jax
import jax.numpy as jnp
from jax import lax
from jax.experimental import pallas as pl
from jax.experimental.pallas import tpu as pltpu
from jax.sharding import PartitionSpec as P

LANES = 128
f32 = jnp.float32
bf16 = jnp.bfloat16


def sine_cosine(angle):
    half = 0.5 * angle
    square = half * half
    sine = jnp.full_like(half, -1.0 / 39916800)
    for term in (1.0 / 362880, -1.0 / 5040, 1.0 / 120, -1.0 / 6, 1.0):
        sine = sine * square + term
    sine = sine * half
    cosine = jnp.full_like(half, 1.0 / 479001600)
    for term in (-1.0 / 3628800, 1.0 / 40320, -1.0 / 720, 1.0 / 24, -0.5, 1.0):
        cosine = cosine * square + term
    return 2.0 * sine * cosine, 1.0 - 2.0 * sine * sine


def build_table(travel_ref, table_ref):
    blocks = travel_ref.shape[1] // LANES

    def step(block, carry):
        start = pl.multiple_of(block * LANES, LANES)
        sine, cosine = sine_cosine(travel_ref[:, pl.ds(start, LANES)])
        table_ref[pl.ds(start, LANES), :] = jnp.concatenate([cosine, sine], axis=0).T
        return carry

    lax.fori_loop(0, blocks, step, 0, unroll=2)


def build_matrix(interp_ref, high_ref, low_ref):
    children = interp_ref.shape[0]
    for k in range(children):
        for c in range(children):
            block = interp_ref[k, c]
            zero = jnp.zeros_like(block)
            block = jnp.concatenate(
                [jnp.concatenate([block, zero], axis=1), jnp.concatenate([zero, block], axis=1)], axis=0
            )
            high = block.astype(bf16)
            where = (slice(k * LANES, (k + 1) * LANES), slice(c * LANES, (c + 1) * LANES))
            high_ref[where] = high
            low_ref[where] = (block - high.astype(f32)).astype(bf16)


def gather_rows(table_ref, row_of, out_ref, start, rows, unroll=16):
    def step(block, carry):
        base = pl.multiple_of(block * unroll, unroll)
        for u in range(unroll):
            out_ref[pl.ds(start + base + u, 1), :] = table_ref[pl.ds(row_of(base + u), 1), :]
        return carry

    lax.fori_loop(0, rows // unroll, step, 0)


def rotate(fields, rotor, sign):
    first = lax.broadcasted_iota(jnp.int32, fields.shape, 1) < LANES // 2
    swapped = pltpu.roll(rotor, LANES // 2, 1)
    cosine = jnp.where(first, rotor, swapped)
    sine = jnp.where(first, swapped * -sign, rotor * sign)
    return fields * cosine + pltpu.roll(fields, LANES // 2, 1) * sine


def store_split(value, high_ref, low_ref, row, column):
    high = value.astype(bf16)
    where = (pl.ds(row, value.shape[0]), pl.ds(column, LANES))
    high_ref[where] = high
    low_ref[where] = (value - high.astype(f32)).astype(bf16)


def product(high, low, matrix_high, matrix_low):
    dot = functools.partial(
        lax.dot_general, dimension_numbers=(((1,), (1,)), ((), ())), preferred_element_type=f32
    )
    return dot(high, matrix_high) + (dot(low, matrix_high) + dot(high, matrix_low))


def first_kernel(weights_ref, interp_ref, travel_ref, entry_ref, exit_ref, out_ref,
                 table_ref, g0, g1, g2, mh, ml, uh, ul):
    count = out_ref.shape[0] // 4
    build_table(travel_ref, table_ref)
    build_matrix(interp_ref, mh, ml)
    gather_rows(table_ref, lambda p: entry_ref[0, p], g0, 0, 4 * count)
    gather_rows(table_ref, lambda p: exit_ref[0, p], g1, 0, 4 * count)
    gather_rows(table_ref, lambda p: entry_ref[1, p], g2, 0, 4 * count)
    blocks = count // LANES
    for block in range(blocks):
        for c in range(4):
            first = (c // 2) * 2 * blocks + block * 2 + c % 2
            field = weights_ref[pl.ds(first, LANES, stride=4 * blocks), :].T
            field = rotate(field, g0[pl.ds(c * count + block * LANES, LANES), :], -1.0)
            store_split(field, uh, ul, 0, c * LANES)
        merged = product(uh[0:LANES, :], ul[0:LANES, :], mh[...], ml[...])
        for k in range(4):
            rows = pl.ds(k * count + block * LANES, LANES)
            value = rotate(merged[:, k * LANES:(k + 1) * LANES], g1[rows, :], 1.0)
            value = rotate(value, g2[rows, :], -1.0)
            out_ref[pl.ds(block * LANES * 4 + k, LANES, stride=4), :] = value


def level_groups(x_size, y_size, bit):
    groups = []
    for i in range(x_size):
        for j in range(y_size):
            if not (i >> bit & 1 or j >> bit & 1):
                groups.append([
                    (i | (c // 2) << bit) * y_size + (j | (c % 2) << bit) for c in range(4)
                ])
    return groups


def last_kernel(x_size, y_size, state_ref, interp_ref, travel_ref, rows_ref, out_ref,
                table_ref, g0, g1, g2, mh, ml, uh, ul, sorted_ref):
    devices = x_size * y_size
    rows = state_ref.shape[0] // devices
    build_table(travel_ref, table_ref)
    build_matrix(interp_ref, mh, ml)
    for which, g in enumerate((g0, g1, g2)):
        gather_rows(table_ref, lambda p, which=which: rows_ref[which, p], g, 0, devices * rows)
    batch = max(1, 256 // rows)
    x_out, y_out = x_size // 4, y_size // 4

    def level(bit, source_ref, finish):
        groups = level_groups(x_size, y_size, bit)
        for start in range(0, len(groups), batch):
            part = groups[start:start + batch]
            for at, group in enumerate(part):
                for c, slot in enumerate(group):
                    store_split(source_ref[pl.ds(slot * rows, rows), :], uh, ul, at * rows, c * LANES)
            size = len(part) * rows
            merged = product(uh[0:size, :], ul[0:size, :], mh[...], ml[...])
            for at, group in enumerate(part):
                for k, slot in enumerate(group):
                    finish(slot, merged[at * rows:(at + 1) * rows, k * LANES:(k + 1) * LANES])

    def finish_first(slot, value):
        where = pl.ds(slot * rows, rows)
        value = rotate(value, g0[where, :], 1.0)
        state_out[where, :] = rotate(value, g1[where, :], -1.0)

    state_out = g0

    def finish_second(slot, value):
        where = pl.ds(slot * rows, rows)
        value = rotate(value, g2[where, :], 1.0)
        i, j = slot // y_size, slot % y_size
        digits = 8 * (i & 1) + 4 * (j & 1) + 2 * (i >> 1 & 1) + (j >> 1 & 1)
        section = (i // 4) * y_out + j // 4
        sorted_ref[pl.ds(section * rows * 16 + digits, rows, stride=16), :] = value

    level(0, state_ref, finish_first)
    level(1, state_out, finish_second)
    blocks = rows * 16 // LANES
    for sx in range(x_out):
        for sy in range(y_out):
            for block in range(blocks):
                start = (sx * y_out + sy) * rows * 16 + block * LANES
                first = (sx * blocks + block) * y_out + sy
                out_ref[pl.ds(first, LANES, stride=x_out * blocks * y_out), :] = (
                    sorted_ref[pl.ds(start, LANES), :].T
                )


def shards(weights, interp, travel, entry_rows, exit_rows):
    count = weights.shape[-1]
    points = interp.shape[-1]
    x_size = lax.axis_size("gx")
    y_size = lax.axis_size("gy")
    devices = x_size * y_size
    share = count // devices
    pairs = 4 * count
    blocks = count // LANES
    vmem = pl.BlockSpec(memory_space=pltpu.VMEM)
    smem = pl.BlockSpec(memory_space=pltpu.SMEM)
    weight_rows = weights.reshape(2, points, 2, 2, blocks, LANES).transpose(0, 1, 2, 4, 3, 5)
    weight_rows = weight_rows.reshape(2 * points * 4 * blocks, LANES)
    rows_array = pltpu.VMEM((pairs, LANES), f32)
    scratch = [
        pltpu.VMEM((travel.shape[1], LANES), f32),
        rows_array, rows_array, rows_array,
        pltpu.VMEM((4 * LANES, 4 * LANES), bf16),
        pltpu.VMEM((4 * LANES, 4 * LANES), bf16),
        pltpu.VMEM((256, 4 * LANES), bf16),
        pltpu.VMEM((256, 4 * LANES), bf16),
    ]
    params = pltpu.CompilerParams(vmem_limit_bytes=48 * 2**20)
    fields = pl.pallas_call(
        first_kernel,
        out_shape=jax.ShapeDtypeStruct((pairs, LANES), f32),
        in_specs=[vmem, vmem, vmem, smem, smem],
        out_specs=vmem,
        scratch_shapes=scratch,
        compiler_params=params,
    )(weight_rows, interp, travel, entry_rows.reshape(3, pairs), exit_rows.reshape(3, pairs))
    state = lax.all_to_all(
        fields.reshape(devices, 4 * share, LANES), ("gx", "gy"), split_axis=0, concat_axis=0, tiled=True
    ).reshape(pairs, LANES)
    tables = jnp.stack([exit_rows[1, 0, 0], entry_rows[2, 0, 0], exit_rows[2, 0, 0]])
    tables = tables.reshape(3, 4, devices, share).transpose(2, 0, 3, 1).reshape(devices, 3 * share * 4)
    tables = lax.all_to_all(tables, ("gx", "gy"), split_axis=0, concat_axis=0, tiled=True)
    tables = tables.reshape(devices, 3, share * 4).transpose(1, 0, 2).reshape(3, pairs)
    x_out, y_out = x_size // 4, y_size // 4
    out_blocks = 64 * share // LANES
    result = pl.pallas_call(
        functools.partial(last_kernel, x_size, y_size),
        out_shape=jax.ShapeDtypeStruct((2 * points * x_out * y_out * out_blocks, LANES), f32),
        in_specs=[vmem, vmem, vmem, smem],
        out_specs=vmem,
        scratch_shapes=scratch + [rows_array],
        compiler_params=params,
    )(state, interp, travel, tables)
    result = result.reshape(2, points, x_out, out_blocks, y_out, LANES).transpose(0, 1, 2, 4, 3, 5)
    return result.reshape(2, points, x_out, y_out, 64 * share)


def solution(mesh):
    return jax.shard_map(
        shards,
        mesh=mesh,
        in_specs=(
            P(None, None, "gx", "gy", None),
            P(),
            P(),
            P(None, "gx", "gy", None),
            P(None, "gx", "gy", None),
        ),
        out_specs=P(None, None, None, None, ("gx", "gy")),
        check_vma=False,
    )
```

profile of v0, /device:TPU:1, one launch (start us, length us, event | category | flops | bytes accessed | tf_op | source)
XLA Modules:
  0.0 89.4 jit_solution(13258778405774067029)
XLA Ops:
  0.0 0.0 copy-start
  0.0 0.9 slice_reduce_fusion.2
  0.9 0.1 stack.11
  1.0 0.1 stack.10
  1.0 0.1 stack.9
  1.1 0.1 copy.14
  1.3 0.7 copy.15
  2.0 0.0 copy-start.4
  2.0 0.0 copy-start.5
  2.0 7.1 %all-to-all-start.1 = ((s32[32,1,192]{2,1,0:T(1,128)}), s32[32,1,192]{2,1,0:T(1,128)S(1)}, u32[]{:S(2)}, u32[]{:S(2)}) async-start(s32[32,1,192]{2,1,0:T(1,128)} %copy.15), calls=%async_computation.1 | async-start | bytes 65536 | tf_op jit(solution)/shard_map/all_to_all | solution.py:209
  9.1 0.0 copy-done.4
  9.1 0.0 copy-done.5
  9.1 0.0 copy-done
  9.1 0.0 copy-start.1
  9.1 1.0 %copy-done.1 = f32[4,4,64,64]{3,2,1,0:T(8,128)S(1)} copy-done((f32[4,4,64,64]{3,2,1,0:T(8,128)S(1)}, f32[4,4,64,64]{3,2,1,0:T(8,128)}, u32[]{:S(2)}) %copy-start.1) | copy-done | bytes 262168
  10.2 0.0 copy-start.3
  10.2 1.2 %copy-done.3 = f32[2,64,2,2,512]{4,3,2,1,0:T(2,128)S(1)} copy-done((f32[2,64,2,2,512]{4,3,2,1,0:T(2,128)S(1)}, f32[2,64,2,2,512]{4,3,2,1,0:T(2,128)}, u32[]{:S(2)}) %copy-start.3) | copy-done | bytes 1048600
  11.4 23.0 %shard_map.55 = f32[2048,128]{1,0:T(8,128)} custom-call(f32[2048,128]{1,0:T(8,128)S(1)} %bitcast.21, f32[4,4,64,64]{3,2,1,0:T(8,128)S(1)} %copy-done.1, f32[64,4096]{1,0:T(8,128)S(1)} %copy-done, s32[3,2048]{1,0:T(4,128)S(1)} %get-tuple-element.8.entry_ref, s32[3,2048]{1,0:T(4,128)S(1)} %get-tuple-element.7.exit_ref), custom_call_target="tpu_custom_call" | custom-call | tf_op jit(solution)/shard_map/pallas_call | solution.py:196
  34.4 0.0 all-to-all-done.1
  34.4 0.0 copy-start.2
  34.4 5.8 %all-to-all-start = ((f32[32,64,128]{2,1,0:T(8,128)}), f32[32,64,128]{2,1,0:T(8,128)S(1)}, u32[]{:S(2)}, u32[]{:S(2)}) async-start(f32[32,64,128]{2,1,0:T(8,128)} %bitcast.3), calls=%async_computation | async-start | bytes 2097152 | tf_op jit(solution)/shard_map/all_to_all | solution.py:204
  40.3 0.1 reduce.3
  40.4 0.1 reshape.48
  40.5 0.1 reshape.49.rows_ref
  40.6 26.7 %all-to-all-done = f32[32,64,128]{2,1,0:T(8,128)S(1)} async-done(((f32[32,64,128]{2,1,0:T(8,128)}), f32[32,64,128]{2,1,0:T(8,128)S(1)}, u32[]{:S(2)}, u32[]{:S(2)}) %all-to-all-start) | async-done | bytes 1048608 | tf_op jit(solution)/shard_map/all_to_all | solution.py:204
  67.3 0.0 copy-done.2
  67.3 22.1 %shard_map.56 = f32[2048,128]{1,0:T(8,128)} custom-call(f32[2048,128]{1,0:T(8,128)S(1)} %bitcast.20, f32[4,4,64,64]{3,2,1,0:T(8,128)S(1)} %copy-done.2, f32[64,4096]{1,0:T(8,128)S(1)} %copy-done, s32[3,2048]{1,0:T(4,128)S(1)} %reshape.49.rows_ref), custom_call_target="tpu_custom_call" | custom-call | tf_op jit(solution)/shard_map/pallas_call | solution.py:213
  (3 shorter events, 0.1 us)
Async XLA Ops:
  0.0 9.1 %copy-start = (f32[64,4096]{1,0:T(8,128)S(1)}, f32[64,4096]{1,0:T(8,128)}, u32[]{:S(2)}) copy-start(f32[64,4096]{1,0:T(8,128)} %travel_ref.3) | copy-start | bytes 3145732
  2.0 7.1 %copy-start.4 = (s32[3,1,1,2048]{3,2,1,0:T(1,128)S(1)}, s32[3,1,1,2048]{3,2,1,0:T(1,128)}, u32[]{:S(2)}) copy-start(s32[3,1,1,2048]{3,2,1,0:T(1,128)} %param.9) | copy-start | bytes 73732
  2.0 7.1 %copy-start.5 = (s32[3,1,1,2048]{3,2,1,0:T(1,128)S(1)}, s32[3,1,1,2048]{3,2,1,0:T(1,128)}, u32[]{:S(2)}) copy-start(s32[3,1,1,2048]{3,2,1,0:T(1,128)} %param.8) | copy-start | bytes 73732
  2.0 32.5 %all-to-all-start.1 = ((s32[32,1,192]{2,1,0:T(1,128)}), s32[32,1,192]{2,1,0:T(1,128)S(1)}, u32[]{:S(2)}, u32[]{:S(2)}) async-start(s32[32,1,192]{2,1,0:T(1,128)} %copy.15), calls=%async_computation.1 | async-start | bytes 65536 | tf_op jit(solution)/shard_map/all_to_all | solution.py:209
  9.1 1.0 %copy-start.1 = (f32[4,4,64,64]{3,2,1,0:T(8,128)S(1)}, f32[4,4,64,64]{3,2,1,0:T(8,128)}, u32[]{:S(2)}) copy-start(f32[4,4,64,64]{3,2,1,0:T(8,128)} %interp_ref.3) | copy-start | bytes 786436
  10.2 1.2 %copy-start.3 = (f32[2,64,2,2,512]{4,3,2,1,0:T(2,128)S(1)}, f32[2,64,2,2,512]{4,3,2,1,0:T(2,128)}, u32[]{:S(2)}) copy-start(f32[2,64,2,2,512]{4,3,2,1,0:T(2,128)} %param.5) | copy-start | bytes 3145732
  34.4 32.8 %copy-start.2 = (f32[4,4,64,64]{3,2,1,0:T(8,128)S(1)}, f32[4,4,64,64]{3,2,1,0:T(8,128)}, u32[]{:S(2)}) copy-start(f32[4,4,64,64]{3,2,1,0:T(8,128)} %interp_ref.3) | copy-start | bytes 786436
  34.4 32.8 %all-to-all-start = ((f32[32,64,128]{2,1,0:T(8,128)}), f32[32,64,128]{2,1,0:T(8,128)S(1)}, u32[]{:S(2)}, u32[]{:S(2)}) async-start(f32[32,64,128]{2,1,0:T(8,128)} %bitcast.3), calls=%async_computation | async-start | bytes 2097152 | tf_op jit(solution)/shard_map/all_to_all | solution.py:204
where the time goes:
time: 90.5 us; the launch traced here: 89.4 us
  Pallas kernels  45.1 us (50%)
  waiting for transfers between devices  26.7 us (30%)
  starting transfers between devices  12.9 us (14%)
  local copies, waits for them, and re-layouts  4.39 us (5%)
    all_to_all x1, waiting for transfers between devices, shards(): lax.all_to_all(fields.reshape(devices, 4 * share, LANES), ('gx', 'gy'), s...  26.7 us
    pallas_call x1, Pallas kernels, shards(): pl.pallas_call(first_kernel, out_shape=jax.ShapeDtypeStruct((pairs, LANES...  23 us
    pallas_call x1, Pallas kernels, shards(): pl.pallas_call(functools.partial(last_kernel, x_size, y_size), out_shape=...  22.1 us
    all_to_all x1, starting transfers between devices, shards(): lax.all_to_all(tables, ('gx', 'gy'), split_axis=0, concat_axis=0, tiled=T...  7.08 us
    all_to_all x1, starting transfers between devices, shards(): lax.all_to_all(fields.reshape(devices, 4 * share, LANES), ('gx', 'gy'), s...  5.84 us
    unnamed x13, local copies, waits for them, and re-layouts  2.3 us
  transfers between devices with their start and end apart: 2, of which 1 were waited for; matrix products, arithmetic and copies ran while one was open for 0% of the time, Pallas kernels for 26%

commit v1 on v0

--- a/solution.py
+++ b/solution.py
@@ -84,29 +84,6 @@
     return dot(high, matrix_high) + (dot(low, matrix_high) + dot(high, matrix_low))
 
 
-def first_kernel(weights_ref, interp_ref, travel_ref, entry_ref, exit_ref, out_ref,
-                 table_ref, g0, g1, g2, mh, ml, uh, ul):
-    count = out_ref.shape[0] // 4
-    build_table(travel_ref, table_ref)
-    build_matrix(interp_ref, mh, ml)
-    gather_rows(table_ref, lambda p: entry_ref[0, p], g0, 0, 4 * count)
-    gather_rows(table_ref, lambda p: exit_ref[0, p], g1, 0, 4 * count)
-    gather_rows(table_ref, lambda p: entry_ref[1, p], g2, 0, 4 * count)
-    blocks = count // LANES
-    for block in range(blocks):
-        for c in range(4):
-            first = (c // 2) * 2 * blocks + block * 2 + c % 2
-            field = weights_ref[pl.ds(first, LANES, stride=4 * blocks), :].T
-            field = rotate(field, g0[pl.ds(c * count + block * LANES, LANES), :], -1.0)
-            store_split(field, uh, ul, 0, c * LANES)
-        merged = product(uh[0:LANES, :], ul[0:LANES, :], mh[...], ml[...])
-        for k in range(4):
-            rows = pl.ds(k * count + block * LANES, LANES)
-            value = rotate(merged[:, k * LANES:(k + 1) * LANES], g1[rows, :], 1.0)
-            value = rotate(value, g2[rows, :], -1.0)
-            out_ref[pl.ds(block * LANES * 4 + k, LANES, stride=4), :] = value
-
-
 def level_groups(x_size, y_size, bit):
     groups = []
     for i in range(x_size):
@@ -118,23 +95,119 @@
     return groups
 
 
-def last_kernel(x_size, y_size, state_ref, interp_ref, travel_ref, rows_ref, out_ref,
-                table_ref, g0, g1, g2, mh, ml, uh, ul, sorted_ref):
+def whole_kernel(x_size, y_size, weights_ref, interp_ref, travel_ref, entry_ref, exit_ref, blocks_ref,
+                 out_ref, table_ref, e0, e1, e2, g0, g1, g2, mh, ml, uh, ul, send_ref, state_ref,
+                 sorted_ref, rows_vmem, rows_smem, row_send, row_recv, data_send, data_recv, smem_sem):
     devices = x_size * y_size
-    rows = state_ref.shape[0] // devices
+    me = lax.axis_index("gx") * y_size + lax.axis_index("gy")
+    pairs = send_ref.shape[0]
+    count = pairs // 4
+    rows = pairs // devices
+    blocks = count // LANES
+    per_block = devices // blocks
+    batch = max(1, 256 // rows)
+    x_out, y_out = x_size // 4, y_size // 4
+
+    def mesh_id(device):
+        return (device // y_size, device % y_size)
+
+    barrier = pltpu.get_barrier_semaphore()
+
+    def greet(step, carry):
+        pl.semaphore_signal(
+            barrier, inc=1, device_id=mesh_id((me + step) % devices),
+            device_id_type=pl.DeviceIdType.MESH,
+        )
+        return carry
+
+    lax.fori_loop(1, devices, greet, 0)
+    own_rows = pltpu.make_async_copy(blocks_ref.at[me], rows_vmem.at[me], row_recv.at[me])
+    own_rows.start()
     build_table(travel_ref, table_ref)
     build_matrix(interp_ref, mh, ml)
-    for which, g in enumerate((g0, g1, g2)):
-        gather_rows(table_ref, lambda p, which=which: rows_ref[which, p], g, 0, devices * rows)
-    batch = max(1, 256 // rows)
-    x_out, y_out = x_size // 4, y_size // 4
-
-    def level(bit, source_ref, finish):
+    pl.semaphore_wait(barrier, devices - 1)
+
+    def row_copy(device):
+        return pltpu.make_async_remote_copy(
+            src_ref=blocks_ref.at[device], dst_ref=rows_vmem.at[me],
+            send_sem=row_send.at[device], recv_sem=row_recv.at[me],
+            device_id=mesh_id(device), device_id_type=pl.DeviceIdType.MESH,
+        )
+
+    def data_copy(device):
+        return pltpu.make_async_remote_copy(
+            src_ref=send_ref.at[pl.ds(pl.multiple_of(device * rows, rows), rows)],
+            dst_ref=state_ref.at[pl.ds(pl.multiple_of(me * rows, rows), rows)],
+            send_sem=data_send.at[device], recv_sem=data_recv.at[me],
+            device_id=mesh_id(device), device_id_type=pl.DeviceIdType.MESH,
+        )
+
+    def each_other(fn):
+        def step(at, carry):
+            fn((me + at) % devices)
+            return carry
+        lax.fori_loop(1, devices, step, 0)
+
+    each_other(lambda device: row_copy(device).start())
+
+    own_slot = pl.ds(pl.multiple_of(me * rows, rows), rows)
+    own_data = pltpu.make_async_copy(send_ref.at[own_slot], state_ref.at[own_slot], data_recv.at[me])
+    for turn in range(blocks):
+        block = (me // per_block + turn) % blocks
+        for c in range(4):
+            base = c * count + block * LANES
+            start = c * LANES
+            gather_rows(table_ref, lambda p: entry_ref[0, base + p], e0, start, LANES)
+            gather_rows(table_ref, lambda p: exit_ref[0, base + p], e1, start, LANES)
+            gather_rows(table_ref, lambda p: entry_ref[1, base + p], e2, start, LANES)
+        for c in range(4):
+            first = (c // 2) * 2 * blocks + block * 2 + c % 2
+            field = weights_ref[pl.ds(first, LANES, stride=4 * blocks), :].T
+            field = rotate(field, e0[c * LANES:(c + 1) * LANES, :], -1.0)
+            store_split(field, uh, ul, 0, c * LANES)
+        merged = product(uh[0:LANES, :], ul[0:LANES, :], mh[...], ml[...])
+        for k in range(4):
+            here = slice(k * LANES, (k + 1) * LANES)
+            value = rotate(merged[:, here], e1[here, :], 1.0)
+            value = rotate(value, e2[here, :], -1.0)
+            send_ref[pl.ds(block * LANES * 4 + k, LANES, stride=4), :] = value
+        if turn == 0:
+            own_data.start()
+
+        def send(at, carry):
+            data_copy(block * per_block + (me + at) % per_block).start()
+            return carry
+
+        lax.fori_loop(1 if turn == 0 else 0, per_block, send, 0)
+
+    def rows_arrived(device, carry):
+        pltpu.make_async_copy(rows_vmem.at[device], rows_vmem.at[device], row_recv.at[device]).wait()
+        return carry
+
+    lax.fori_loop(0, devices, rows_arrived, 0)
+    to_smem = pltpu.make_async_copy(rows_vmem, rows_smem, smem_sem)
+    to_smem.start()
+    to_smem.wait()
+
+    def later_rows(device, carry):
+        base = pl.multiple_of(device * rows, rows)
+        for which, g in enumerate((g0, g1, g2)):
+            for at in range(rows):
+                row = rows_smem[device, 0, which * rows + at]
+                g[pl.ds(base + at, 1), :] = table_ref[pl.ds(row, 1), :]
+        here = pl.ds(base, rows)
+        g0[here, :] = rotate(g0[here, :], g1[here, :], -1.0)
+        return carry
+
+    lax.fori_loop(0, devices, later_rows, 0)
+
+    def level(bit, source_ref, finish, arrived):
         groups = level_groups(x_size, y_size, bit)
         for start in range(0, len(groups), batch):
             part = groups[start:start + batch]
             for at, group in enumerate(part):
                 for c, slot in enumerate(group):
+                    arrived(slot)
                     store_split(source_ref[pl.ds(slot * rows, rows), :], uh, ul, at * rows, c * LANES)
             size = len(part) * rows
             merged = product(uh[0:size, :], ul[0:size, :], mh[...], ml[...])
@@ -144,10 +217,7 @@
 
     def finish_first(slot, value):
         where = pl.ds(slot * rows, rows)
-        value = rotate(value, g0[where, :], 1.0)
-        state_out[where, :] = rotate(value, g1[where, :], -1.0)
-
-    state_out = g0
+        g1[where, :] = rotate(value, g0[where, :], 1.0)
 
     def finish_second(slot, value):
         where = pl.ds(slot * rows, rows)
@@ -157,17 +227,23 @@
         section = (i // 4) * y_out + j // 4
         sorted_ref[pl.ds(section * rows * 16 + digits, rows, stride=16), :] = value
 
-    level(0, state_ref, finish_first)
-    level(1, state_out, finish_second)
-    blocks = rows * 16 // LANES
+    def data_arrived(slot):
+        where = state_ref.at[pl.ds(slot * rows, rows)]
+        pltpu.make_async_copy(where, where, data_recv.at[slot]).wait()
+
+    level(0, state_ref, finish_first, data_arrived)
+    level(1, g1, finish_second, lambda slot: None)
+    out_blocks = rows * 16 // LANES
     for sx in range(x_out):
         for sy in range(y_out):
-            for block in range(blocks):
+            for block in range(out_blocks):
                 start = (sx * y_out + sy) * rows * 16 + block * LANES
-                first = (sx * blocks + block) * y_out + sy
-                out_ref[pl.ds(first, LANES, stride=x_out * blocks * y_out), :] = (
+                first = (sx * out_blocks + block) * y_out + sy
+                out_ref[pl.ds(first, LANES, stride=x_out * out_blocks * y_out), :] = (
                     sorted_ref[pl.ds(start, LANES), :].T
                 )
+    each_other(lambda device: row_copy(device).wait_send())
+    each_other(lambda device: data_copy(device).wait_send())
 
 
 def shards(weights, interp, travel, entry_rows, exit_rows):
@@ -183,41 +259,37 @@
     smem = pl.BlockSpec(memory_space=pltpu.SMEM)
     weight_rows = weights.reshape(2, points, 2, 2, blocks, LANES).transpose(0, 1, 2, 4, 3, 5)
     weight_rows = weight_rows.reshape(2 * points * 4 * blocks, LANES)
-    rows_array = pltpu.VMEM((pairs, LANES), f32)
-    scratch = [
-        pltpu.VMEM((travel.shape[1], LANES), f32),
-        rows_array, rows_array, rows_array,
-        pltpu.VMEM((4 * LANES, 4 * LANES), bf16),
-        pltpu.VMEM((4 * LANES, 4 * LANES), bf16),
-        pltpu.VMEM((256, 4 * LANES), bf16),
-        pltpu.VMEM((256, 4 * LANES), bf16),
-    ]
-    params = pltpu.CompilerParams(vmem_limit_bytes=48 * 2**20)
-    fields = pl.pallas_call(
-        first_kernel,
-        out_shape=jax.ShapeDtypeStruct((pairs, LANES), f32),
-        in_specs=[vmem, vmem, vmem, smem, smem],
-        out_specs=vmem,
-        scratch_shapes=scratch,
-        compiler_params=params,
-    )(weight_rows, interp, travel, entry_rows.reshape(3, pairs), exit_rows.reshape(3, pairs))
-    state = lax.all_to_all(
-        fields.reshape(devices, 4 * share, LANES), ("gx", "gy"), split_axis=0, concat_axis=0, tiled=True
-    ).reshape(pairs, LANES)
     tables = jnp.stack([exit_rows[1, 0, 0], entry_rows[2, 0, 0], exit_rows[2, 0, 0]])
     tables = tables.reshape(3, 4, devices, share).transpose(2, 0, 3, 1).reshape(devices, 3 * share * 4)
-    tables = lax.all_to_all(tables, ("gx", "gy"), split_axis=0, concat_axis=0, tiled=True)
-    tables = tables.reshape(devices, 3, share * 4).transpose(1, 0, 2).reshape(3, pairs)
+    width = -(-3 * share * 4 // LANES) * LANES
+    tables = jnp.pad(tables, ((0, 0), (0, width - 3 * share * 4))).reshape(devices, 1, width)
+    rows_array = pltpu.VMEM((pairs, LANES), f32)
+    block_rows = pltpu.VMEM((4 * LANES, LANES), f32)
+    matrix = pltpu.VMEM((4 * LANES, 4 * LANES), bf16)
+    operand = pltpu.VMEM((256, 4 * LANES), bf16)
     x_out, y_out = x_size // 4, y_size // 4
     out_blocks = 64 * share // LANES
+    semaphores = pltpu.SemaphoreType.DMA((devices,))
     result = pl.pallas_call(
-        functools.partial(last_kernel, x_size, y_size),
+        functools.partial(whole_kernel, x_size, y_size),
         out_shape=jax.ShapeDtypeStruct((2 * points * x_out * y_out * out_blocks, LANES), f32),
-        in_specs=[vmem, vmem, vmem, smem],
+        in_specs=[vmem, vmem, vmem, smem, smem, vmem],
         out_specs=vmem,
-        scratch_shapes=scratch + [rows_array],
-        compiler_params=params,
-    )(state, interp, travel, tables)
+        scratch_shapes=[
+            pltpu.VMEM((travel.shape[1], LANES), f32),
+            block_rows, block_rows, block_rows,
+            rows_array, rows_array, rows_array,
+            matrix, matrix, operand, operand,
+            rows_array, rows_array, rows_array,
+            pltpu.VMEM((devices, 1, width), jnp.int32),
+            pltpu.SMEM((devices, 1, width), jnp.int32),
+            semaphores, semaphores, semaphores, semaphores,
+            pltpu.SemaphoreType.DMA,
+        ],
+        compiler_params=pltpu.CompilerParams(
+            vmem_limit_bytes=48 * 2**20, collective_id=0, has_side_effects=True
+        ),
+    )(weight_rows, interp, travel, entry_rows.reshape(3, pairs), exit_rows.reshape(3, pairs), tables)
     result = result.reshape(2, points, x_out, out_blocks, y_out, LANES).transpose(0, 1, 2, 4, 3, 5)
     return result.reshape(2, points, x_out, y_out, 64 * share)
 

time: 90.5 us -> 49.1 us (0.54)
  waiting for transfers between devices: 26.7 us -> 0 us
  starting transfers between devices: 12.9 us -> 0 us
  Pallas kernels: 45.1 us -> 43.3 us
    all_to_all x2 -> x0, waiting for transfers between devices: 26.7 us -> none  [the longest x1 26.7 us: shards(): lax.all_to_all(fields.reshape(devices, 4 * share, LANES), ('gx', 'gy'), s...]
    all_to_all x2 -> x0, starting transfers between devices: 12.9 us -> none  [the longest x1 7.08 us: shards(): lax.all_to_all(tables, ('gx', 'gy'), split_axis=0, concat_axis=0, tiled=T...]
    pallas_call x2 -> x1, Pallas kernels: 45.1 us -> 43.3 us  [shards(): pl.pallas_call(functools.partial(whole_kernel, x_size, y_size), out_shape...]
    unnamed x13 -> x12, local copies, waits for them, and re-layouts: 2.3 us -> 3.97 us
  transfers between devices with their start and end apart: 2 -> 0, of which waited for: 1 -> 0; matrix products, arithmetic and copies ran while one was open for 0% -> 0% of each run, Pallas kernels for 26% -> 0%
where the time goes in v1:
time: 49.1 us; the launch traced here: 48.7 us
  Pallas kernels  43.3 us (88%)
  local copies, waits for them, and re-layouts  5.28 us (11%)
    pallas_call x1, Pallas kernels, shards(): pl.pallas_call(functools.partial(whole_kernel, x_size, y_size), out_shape...  43.3 us
    unnamed x12, local copies, waits for them, and re-layouts  3.97 us

profile of v1, /device:TPU:1, one launch (start us, length us, event | category | flops | bytes accessed | tf_op | source)
XLA Modules:
  0.0 48.7 jit_solution(5194281714271432031)
XLA Ops:
  0.0 0.0 copy-start
  0.0 0.9 %slice_reduce_fusion.2 = (s32[2048]{0:T(1024)S(1)}, s32[2048]{0:T(1024)S(1)}, s32[2048]{0:T(1024)S(1)}) fusion(s32[3,1,1,2048]{3,2,1,0:T(1,128)} %param.9, s32[3,1,1,2048]{3,2,1,0:T(1,128)} %param.8), kind=kLoop, calls=%fused_computation.5 | loop fusion | bytes 49152 | tf_op jit(solution)/shard_map/slice | solution.py:262
  0.9 0.1 stack.9
  1.0 0.1 stack.11
  1.0 0.1 stack.10
  1.1 0.1 copy.12
  1.3 0.1 copy.13
  1.4 0.0 copy-start.3
  1.4 0.0 copy-start.4
  1.4 0.7 %copy-done.3 = s32[3,1,1,2048]{3,2,1,0:T(1,128)S(1)} copy-done((s32[3,1,1,2048]{3,2,1,0:T(1,128)S(1)}, s32[3,1,1,2048]{3,2,1,0:T(1,128)}, u32[]{:S(2)}) %copy-start.3) | copy-done | bytes 24600
  2.1 0.0 copy-done.4
  2.1 0.0 copy-done
  2.2 0.0 copy-start.1
  2.2 1.2 %copy-done.1 = f32[64,4096]{1,0:T(8,128)S(1)} copy-done((f32[64,4096]{1,0:T(8,128)S(1)}, f32[64,4096]{1,0:T(8,128)}, u32[]{:S(2)}) %copy-start.1) | copy-done | bytes 1048600
  3.4 0.0 copy-start.2
  3.4 1.0 %copy-done.2 = f32[4,4,64,64]{3,2,1,0:T(8,128)S(1)} copy-done((f32[4,4,64,64]{3,2,1,0:T(8,128)S(1)}, f32[4,4,64,64]{3,2,1,0:T(8,128)}, u32[]{:S(2)}) %copy-start.2) | copy-done | bytes 262168
  4.4 43.3 %shard_map.55 = f32[2048,128]{1,0:T(8,128)S(1)} custom-call(f32[2048,128]{1,0:T(8,128)S(1)} %bitcast.18, f32[4,4,64,64]{3,2,1,0:T(8,128)S(1)} %copy-done.2, f32[64,4096]{1,0:T(8,128)S(1)} %copy-done.1, s32[3,2048]{1,0:T(4,128)S(1)} %get-tuple-element.9.entry_ref, s32[3,2048]{1,0:T(4,128)S(1)} %get-tuple-element.8.exit_ref, s32[32,1,256]{2,1,0:T(1,128)S(1)} %reshape.36.blocks_ref), custom_call_target="tpu_custom_call" | custom-call | tf_op jit(solution)/shard_map/pallas_call | solution.py:273
  47.7 1.0 %copy.20 = f32[2,64,1,2,1024]{4,3,2,1,0:T(2,128)} copy(f32[2,64,1,2,1024]{4,3,2,1,0:T(2,128)S(1)} %bitcast.17) | data formatting | bytes 2097152
  (4 shorter events, 0.1 us)
Async XLA Ops:
  0.0 2.1 %copy-start = (f32[2,64,2,2,512]{4,3,2,1,0:T(2,128)S(1)}, f32[2,64,2,2,512]{4,3,2,1,0:T(2,128)}, u32[]{:S(2)}) copy-start(f32[2,64,2,2,512]{4,3,2,1,0:T(2,128)} %param.5) | copy-start | bytes 3145732
  1.4 0.7 %copy-start.3 = (s32[3,1,1,2048]{3,2,1,0:T(1,128)S(1)}, s32[3,1,1,2048]{3,2,1,0:T(1,128)}, u32[]{:S(2)}) copy-start(s32[3,1,1,2048]{3,2,1,0:T(1,128)} %param.9) | copy-start | bytes 73732
  1.4 0.7 %copy-start.4 = (s32[3,1,1,2048]{3,2,1,0:T(1,128)S(1)}, s32[3,1,1,2048]{3,2,1,0:T(1,128)}, u32[]{:S(2)}) copy-start(s32[3,1,1,2048]{3,2,1,0:T(1,128)} %param.8) | copy-start | bytes 73732
  2.2 1.2 %copy-start.1 = (f32[64,4096]{1,0:T(8,128)S(1)}, f32[64,4096]{1,0:T(8,128)}, u32[]{:S(2)}) copy-start(f32[64,4096]{1,0:T(8,128)} %travel_ref.1) | copy-start | bytes 3145732
  3.4 1.0 %copy-start.2 = (f32[4,4,64,64]{3,2,1,0:T(8,128)S(1)}, f32[4,4,64,64]{3,2,1,0:T(8,128)}, u32[]{:S(2)}) copy-start(f32[4,4,64,64]{3,2,1,0:T(8,128)} %interp_ref.1) | copy-start | bytes 786436

commit v2 on v1

--- a/solution.py
+++ b/solution.py
@@ -52,16 +52,6 @@
             low_ref[where] = (block - high.astype(f32)).astype(bf16)
 
 
-def gather_rows(table_ref, row_of, out_ref, start, rows, unroll=16):
-    def step(block, carry):
-        base = pl.multiple_of(block * unroll, unroll)
-        for u in range(unroll):
-            out_ref[pl.ds(start + base + u, 1), :] = table_ref[pl.ds(row_of(base + u), 1), :]
-        return carry
-
-    lax.fori_loop(0, rows // unroll, step, 0)
-
-
 def rotate(fields, rotor, sign):
     first = lax.broadcasted_iota(jnp.int32, fields.shape, 1) < LANES // 2
     swapped = pltpu.roll(rotor, LANES // 2, 1)
@@ -153,13 +143,19 @@
     own_slot = pl.ds(pl.multiple_of(me * rows, rows), rows)
     own_data = pltpu.make_async_copy(send_ref.at[own_slot], state_ref.at[own_slot], data_recv.at[me])
     for turn in range(blocks):
-        block = (me // per_block + turn) % blocks
-        for c in range(4):
-            base = c * count + block * LANES
-            start = c * LANES
-            gather_rows(table_ref, lambda p: entry_ref[0, base + p], e0, start, LANES)
-            gather_rows(table_ref, lambda p: exit_ref[0, base + p], e1, start, LANES)
-            gather_rows(table_ref, lambda p: entry_ref[1, base + p], e2, start, LANES)
+        own = me // per_block
+        block = (own // 2 + turn // 2) % (blocks // 2) * 2 + (own % 2 + turn % 2) % 2
+
+        def early_rows(c, carry, block=block):
+            start = pl.multiple_of(c * LANES, LANES)
+            at_block = c * blocks + block
+            for table, which, out in ((entry_ref, 0, e0), (exit_ref, 0, e1), (entry_ref, 1, e2)):
+                for at in range(LANES):
+                    row = table[which * 4 * blocks + at_block, 0, at]
+                    out[pl.ds(start + at, 1), :] = table_ref[pl.ds(row, 1), :]
+            return carry
+
+        lax.fori_loop(0, 4, early_rows, 0)
         for c in range(4):
             first = (c // 2) * 2 * blocks + block * 2 + c % 2
             field = weights_ref[pl.ds(first, LANES, stride=4 * blocks), :].T
@@ -201,13 +197,12 @@
 
     lax.fori_loop(0, devices, later_rows, 0)
 
-    def level(bit, source_ref, finish, arrived):
+    def level(bit, source_ref, finish):
         groups = level_groups(x_size, y_size, bit)
         for start in range(0, len(groups), batch):
             part = groups[start:start + batch]
             for at, group in enumerate(part):
                 for c, slot in enumerate(group):
-                    arrived(slot)
                     store_split(source_ref[pl.ds(slot * rows, rows), :], uh, ul, at * rows, c * LANES)
             size = len(part) * rows
             merged = product(uh[0:size, :], ul[0:size, :], mh[...], ml[...])
@@ -215,9 +210,27 @@
                 for k, slot in enumerate(group):
                     finish(slot, merged[at * rows:(at + 1) * rows, k * LANES:(k + 1) * LANES])
 
-    def finish_first(slot, value):
-        where = pl.ds(slot * rows, rows)
-        g1[where, :] = rotate(value, g0[where, :], 1.0)
+    def slot_rows(slot):
+        return pl.ds(pl.multiple_of(slot * rows, rows), rows)
+
+    x_pairs, y_pairs = x_size // 2, y_size // 2
+    for turn in range(x_pairs):
+        x_pair = (lax.axis_index("gx") // 2 + turn) % x_pairs
+        groups = [
+            [(2 * x_pair + c // 2) * y_size + 2 * y_pair + c % 2 for c in range(4)]
+            for y_pair in range(y_pairs)
+        ]
+        for at, group in enumerate(groups):
+            for c, slot in enumerate(group):
+                arriving = state_ref.at[slot_rows(slot)]
+                pltpu.make_async_copy(arriving, arriving, data_recv.at[slot]).wait()
+                store_split(state_ref[slot_rows(slot), :], uh, ul, at * rows, c * LANES)
+        size = y_pairs * rows
+        merged = product(uh[0:size, :], ul[0:size, :], mh[...], ml[...])
+        for at, group in enumerate(groups):
+            for k, slot in enumerate(group):
+                value = merged[at * rows:(at + 1) * rows, k * LANES:(k + 1) * LANES]
+                g1[slot_rows(slot), :] = rotate(value, g0[slot_rows(slot), :], 1.0)
 
     def finish_second(slot, value):
         where = pl.ds(slot * rows, rows)
@@ -227,12 +240,7 @@
         section = (i // 4) * y_out + j // 4
         sorted_ref[pl.ds(section * rows * 16 + digits, rows, stride=16), :] = value
 
-    def data_arrived(slot):
-        where = state_ref.at[pl.ds(slot * rows, rows)]
-        pltpu.make_async_copy(where, where, data_recv.at[slot]).wait()
-
-    level(0, state_ref, finish_first, data_arrived)
-    level(1, g1, finish_second, lambda slot: None)
+    level(1, g1, finish_second)
     out_blocks = rows * 16 // LANES
     for sx in range(x_out):
         for sy in range(y_out):
@@ -266,7 +274,7 @@
     rows_array = pltpu.VMEM((pairs, LANES), f32)
     block_rows = pltpu.VMEM((4 * LANES, LANES), f32)
     matrix = pltpu.VMEM((4 * LANES, 4 * LANES), bf16)
-    operand = pltpu.VMEM((256, 4 * LANES), bf16)
+    operand = pltpu.VMEM((max(256, y_size // 2 * 4 * share), 4 * LANES), bf16)
     x_out, y_out = x_size // 4, y_size // 4
     out_blocks = 64 * share // LANES
     semaphores = pltpu.SemaphoreType.DMA((devices,))
@@ -289,7 +297,7 @@
         compiler_params=pltpu.CompilerParams(
             vmem_limit_bytes=48 * 2**20, collective_id=0, has_side_effects=True
         ),
-    )(weight_rows, interp, travel, entry_rows.reshape(3, pairs), exit_rows.reshape(3, pairs), tables)
+    )(weight_rows, interp, travel, entry_rows.reshape(3 * 4 * blocks, 1, LANES), exit_rows.reshape(3 * 4 * blocks, 1, LANES), tables)
     result = result.reshape(2, points, x_out, out_blocks, y_out, LANES).transpose(0, 1, 2, 4, 3, 5)
     return result.reshape(2, points, x_out, y_out, 64 * share)
 

time: 49.1 us -> 44.7 us (0.910)
  Pallas kernels: 43.3 us -> 39.1 us
    pallas_call x1, Pallas kernels: 43.3 us -> 39.1 us  [shards(): pl.pallas_call(functools.partial(whole_kernel, x_size, y_size), out_shape...]
    unnamed x12 -> x11, local copies, waits for them, and re-layouts: 3.97 us -> 3.94 us
where the time goes in v2:
time: 44.7 us; the launch traced here: 44.5 us
  Pallas kernels  39.1 us (87%)
  local copies, waits for them, and re-layouts  5.25 us (12%)
    pallas_call x1, Pallas kernels, shards(): pl.pallas_call(functools.partial(whole_kernel, x_size, y_size), out_shape...  39.1 us
    unnamed x11, local copies, waits for them, and re-layouts  3.94 us

profile of v2, /device:TPU:1, one launch (start us, length us, event | category | flops | bytes accessed | tf_op | source)
XLA Modules:
  0.0 44.5 jit_solution(5313118940141252344)
XLA Ops:
  0.0 0.0 copy-start
  0.0 0.9 %slice_reduce_fusion.2 = (s32[2048]{0:T(1024)S(1)}, s32[2048]{0:T(1024)S(1)}, s32[2048]{0:T(1024)S(1)}) fusion(s32[3,1,1,2048]{3,2,1,0:T(1,128)} %param.9, s32[3,1,1,2048]{3,2,1,0:T(1,128)} %param.8), kind=kLoop, calls=%fused_computation.3 | loop fusion | bytes 49152 | tf_op jit(solution)/shard_map/slice | solution.py:270
  0.9 0.1 stack.9
  1.0 0.1 stack.11
  1.0 0.1 stack.10
  1.1 0.1 copy.12
  1.3 0.1 copy.13
  1.4 0.0 copy-start.3
  1.4 0.0 copy-start.4
  1.4 0.0 copy-done
  1.4 0.7 %copy-done.3 = s32[3,1,1,2048]{3,2,1,0:T(1,128)S(1)} copy-done((s32[3,1,1,2048]{3,2,1,0:T(1,128)S(1)}, s32[3,1,1,2048]{3,2,1,0:T(1,128)}, u32[]{:S(2)}) %copy-start.3) | copy-done | bytes 24600
  2.1 0.0 copy-done.4
  2.1 0.0 copy-start.1
  2.1 1.2 %copy-done.1 = f32[64,4096]{1,0:T(8,128)S(1)} copy-done((f32[64,4096]{1,0:T(8,128)S(1)}, f32[64,4096]{1,0:T(8,128)}, u32[]{:S(2)}) %copy-start.1) | copy-done | bytes 1048600
  3.3 0.0 copy-start.2
  3.3 1.0 %copy-done.2 = f32[4,4,64,64]{3,2,1,0:T(8,128)S(1)} copy-done((f32[4,4,64,64]{3,2,1,0:T(8,128)S(1)}, f32[4,4,64,64]{3,2,1,0:T(8,128)}, u32[]{:S(2)}) %copy-start.2) | copy-done | bytes 262168
  4.4 39.1 %shard_map.55 = f32[2048,128]{1,0:T(8,128)S(1)} custom-call(f32[2048,128]{1,0:T(8,128)S(1)} %bitcast.16, f32[4,4,64,64]{3,2,1,0:T(8,128)S(1)} %copy-done.2, f32[64,4096]{1,0:T(8,128)S(1)} %copy-done.1, s32[48,1,128]{2,1,0:T(1,128)S(1)} %bitcast.18, s32[48,1,128]{2,1,0:T(1,128)S(1)} %bitcast.17, s32[32,1,256]{2,1,0:T(1,128)S(1)} %reshape.36.blocks_ref), custom_call_target="tpu_custom_call" | custom-call | tf_op jit(solution)/shard_map/pallas_call | solution.py:281
  43.5 1.0 %copy.16 = f32[2,64,1,2,1024]{4,3,2,1,0:T(2,128)} copy(f32[2,64,1,2,1024]{4,3,2,1,0:T(2,128)S(1)} %bitcast.15) | data formatting | bytes 2097152
  (3 shorter events, 0.1 us)
Async XLA Ops:
  0.0 1.4 %copy-start = (f32[2,64,2,2,512]{4,3,2,1,0:T(2,128)S(1)}, f32[2,64,2,2,512]{4,3,2,1,0:T(2,128)}, u32[]{:S(2)}) copy-start(f32[2,64,2,2,512]{4,3,2,1,0:T(2,128)} %param.5) | copy-start | bytes 3145732
  1.4 0.7 %copy-start.3 = (s32[3,1,1,2048]{3,2,1,0:T(1,128)S(1)}, s32[3,1,1,2048]{3,2,1,0:T(1,128)}, u32[]{:S(2)}) copy-start(s32[3,1,1,2048]{3,2,1,0:T(1,128)} %param.9) | copy-start | bytes 73732
  1.4 0.7 %copy-start.4 = (s32[3,1,1,2048]{3,2,1,0:T(1,128)S(1)}, s32[3,1,1,2048]{3,2,1,0:T(1,128)}, u32[]{:S(2)}) copy-start(s32[3,1,1,2048]{3,2,1,0:T(1,128)} %param.8) | copy-start | bytes 73732
  2.1 1.2 %copy-start.1 = (f32[64,4096]{1,0:T(8,128)S(1)}, f32[64,4096]{1,0:T(8,128)}, u32[]{:S(2)}) copy-start(f32[64,4096]{1,0:T(8,128)} %travel_ref.1) | copy-start | bytes 3145732
  3.3 1.0 %copy-start.2 = (f32[4,4,64,64]{3,2,1,0:T(8,128)S(1)}, f32[4,4,64,64]{3,2,1,0:T(8,128)}, u32[]{:S(2)}) copy-start(f32[4,4,64,64]{3,2,1,0:T(8,128)} %interp_ref.1) | copy-start | bytes 786436

commit v3 on v2

--- a/solution.py
+++ b/solution.py
@@ -85,9 +85,10 @@
     return groups
 
 
-def whole_kernel(x_size, y_size, weights_ref, interp_ref, travel_ref, entry_ref, exit_ref, blocks_ref,
+def whole_kernel(x_size, y_size, weights_hbm, interp_hbm, travel_hbm, entry_ref, exit_ref, blocks_ref,
                  out_ref, table_ref, e0, e1, e2, g0, g1, g2, mh, ml, uh, ul, send_ref, state_ref,
-                 sorted_ref, rows_vmem, rows_smem, row_send, row_recv, data_send, data_recv, smem_sem):
+                 sorted_ref, rows_vmem, rows_smem, row_send, row_recv, data_send, data_recv, smem_sem,
+                 weights_ref, interp_ref, travel_ref, load_sem):
     devices = x_size * y_size
     me = lax.axis_index("gx") * y_size + lax.axis_index("gy")
     pairs = send_ref.shape[0]
@@ -101,6 +102,12 @@
     def mesh_id(device):
         return (device // y_size, device % y_size)
 
+    load_travel = pltpu.make_async_copy(travel_hbm, travel_ref, load_sem.at[0])
+    load_interp = pltpu.make_async_copy(interp_hbm, interp_ref, load_sem.at[1])
+    load_weights = pltpu.make_async_copy(weights_hbm, weights_ref, load_sem.at[2])
+    load_travel.start()
+    load_interp.start()
+    load_weights.start()
     barrier = pltpu.get_barrier_semaphore()
 
     def greet(step, carry):
@@ -113,9 +120,11 @@
     lax.fori_loop(1, devices, greet, 0)
     own_rows = pltpu.make_async_copy(blocks_ref.at[me], rows_vmem.at[me], row_recv.at[me])
     own_rows.start()
+    load_travel.wait()
     build_table(travel_ref, table_ref)
+    load_interp.wait()
     build_matrix(interp_ref, mh, ml)
-    pl.semaphore_wait(barrier, devices - 1)
+    load_weights.wait()
 
     def row_copy(device):
         return pltpu.make_async_remote_copy(
@@ -137,8 +146,6 @@
             fn((me + at) % devices)
             return carry
         lax.fori_loop(1, devices, step, 0)
-
-    each_other(lambda device: row_copy(device).start())
 
     own_slot = pl.ds(pl.multiple_of(me * rows, rows), rows)
     own_data = pltpu.make_async_copy(send_ref.at[own_slot], state_ref.at[own_slot], data_recv.at[me])
@@ -169,6 +176,8 @@
             send_ref[pl.ds(block * LANES * 4 + k, LANES, stride=4), :] = value
         if turn == 0:
             own_data.start()
+            pl.semaphore_wait(barrier, devices - 1)
+            each_other(lambda device: row_copy(device).start())
 
         def send(at, carry):
             data_copy(block * per_block + (me + at) % per_block).start()
@@ -265,6 +274,7 @@
     blocks = count // LANES
     vmem = pl.BlockSpec(memory_space=pltpu.VMEM)
     smem = pl.BlockSpec(memory_space=pltpu.SMEM)
+    hbm = pl.BlockSpec(memory_space=pltpu.HBM)
     weight_rows = weights.reshape(2, points, 2, 2, blocks, LANES).transpose(0, 1, 2, 4, 3, 5)
     weight_rows = weight_rows.reshape(2 * points * 4 * blocks, LANES)
     tables = jnp.stack([exit_rows[1, 0, 0], entry_rows[2, 0, 0], exit_rows[2, 0, 0]])
@@ -281,7 +291,7 @@
     result = pl.pallas_call(
         functools.partial(whole_kernel, x_size, y_size),
         out_shape=jax.ShapeDtypeStruct((2 * points * x_out * y_out * out_blocks, LANES), f32),
-        in_specs=[vmem, vmem, vmem, smem, smem, vmem],
+        in_specs=[hbm, hbm, hbm, smem, smem, vmem],
         out_specs=vmem,
         scratch_shapes=[
             pltpu.VMEM((travel.shape[1], LANES), f32),
@@ -293,9 +303,13 @@
             pltpu.SMEM((devices, 1, width), jnp.int32),
             semaphores, semaphores, semaphores, semaphores,
             pltpu.SemaphoreType.DMA,
+            pltpu.VMEM(weight_rows.shape, f32),
+            pltpu.VMEM(interp.shape, f32),
+            pltpu.VMEM(travel.shape, f32),
+            pltpu.SemaphoreType.DMA((3,)),
         ],
         compiler_params=pltpu.CompilerParams(
-            vmem_limit_bytes=48 * 2**20, collective_id=0, has_side_effects=True
+            vmem_limit_bytes=64000000, collective_id=0, has_side_effects=True
         ),
     )(weight_rows, interp, travel, entry_rows.reshape(3 * 4 * blocks, 1, LANES), exit_rows.reshape(3 * 4 * blocks, 1, LANES), tables)
     result = result.reshape(2, points, x_out, out_blocks, y_out, LANES).transpose(0, 1, 2, 4, 3, 5)

time: 44.7 us -> 45.4 us (1.016)
  Pallas kernels: 39.1 us -> 40.9 us
  local copies, waits for them, and re-layouts: 5.25 us -> 4.1 us
    pallas_call x1, Pallas kernels: 39.1 us -> 40.9 us  [shards(): pl.pallas_call(functools.partial(whole_kernel, x_size, y_size), out_shape...]
    unnamed x11 -> x1, local copies, waits for them, and re-layouts: 3.94 us -> 2.26 us
    reshape x1, local copies, waits for them, and re-layouts: 0.02 us -> 0.64 us  [shards(): jnp.pad(tables, ((0, 0), (0, width - 3 * share * 4)))]
where the time goes in v3:
time: 45.4 us; the launch traced here: 45.1 us
  Pallas kernels  40.9 us (90%)
  local copies, waits for them, and re-layouts  4.1 us (9%)
    pallas_call x1, Pallas kernels, shards(): pl.pallas_call(functools.partial(whole_kernel, x_size, y_size), out_shape...  40.9 us
    unnamed x1, local copies, waits for them, and re-layouts  2.26 us

profile of v3, /device:TPU:1, one launch (start us, length us, event | category | flops | bytes accessed | tf_op | source)
XLA Modules:
  0.0 45.1 jit_solution(5245540304119166447)
XLA Ops:
  0.0 0.8 %slice_reduce_fusion.2 = (s32[2048]{0:T(1024)S(1)}, s32[2048]{0:T(1024)S(1)}, s32[2048]{0:T(1024)S(1)}) fusion(s32[3,1,1,2048]{3,2,1,0:T(1,128)} %param.9, s32[3,1,1,2048]{3,2,1,0:T(1,128)} %param.8), kind=kLoop, calls=%fused_computation.3 | loop fusion | bytes 49152 | tf_op jit(solution)/shard_map/slice | solution.py:280
  0.8 0.1 stack.9
  0.9 0.1 stack.11
  0.9 0.1 stack.10
  1.1 0.1 copy.12
  1.2 0.1 copy.13
  1.3 0.6 %reshape.36.blocks_ref = s32[32,1,256]{2,1,0:T(1,128)} reshape(s32[32,256]{1,0:T(8,128)S(1)} %pad.4) | data formatting | bytes 65536 | tf_op jit(solution)/shard_map/reshape | solution.py:283
  1.9 40.9 %shard_map.55 = f32[2048,128]{1,0:T(8,128)} custom-call(f32[2048,128]{1,0:T(8,128)} %bitcast.16, f32[4,4,64,64]{3,2,1,0:T(8,128)} %interp_hbm.1, f32[64,4096]{1,0:T(8,128)} %travel_hbm.1, s32[48,1,128]{2,1,0:T(1,128)} %bitcast.19, s32[48,1,128]{2,1,0:T(1,128)} %bitcast.18, s32[32,1,256]{2,1,0:T(1,128)} %reshape.36.blocks_ref), custom_call_target="tpu_custom_call" | custom-call | tf_op jit(solution)/shard_map/pallas_call | solution.py:291
  42.8 2.3 %copy.16 = f32[2,64,1,2,1024]{4,3,2,1,0:T(2,128)} copy(f32[2,64,1,2,1024]{4,3,2,1,0:T(2,128)} %bitcast.15) | data formatting | bytes 2097152
  (2 shorter events, 0.0 us)

commit v4 on v2

--- a/solution.py
+++ b/solution.py
@@ -115,7 +115,6 @@
     own_rows.start()
     build_table(travel_ref, table_ref)
     build_matrix(interp_ref, mh, ml)
-    pl.semaphore_wait(barrier, devices - 1)
 
     def row_copy(device):
         return pltpu.make_async_remote_copy(
@@ -137,8 +136,6 @@
             fn((me + at) % devices)
             return carry
         lax.fori_loop(1, devices, step, 0)
-
-    each_other(lambda device: row_copy(device).start())
 
     own_slot = pl.ds(pl.multiple_of(me * rows, rows), rows)
     own_data = pltpu.make_async_copy(send_ref.at[own_slot], state_ref.at[own_slot], data_recv.at[me])
@@ -169,6 +166,8 @@
             send_ref[pl.ds(block * LANES * 4 + k, LANES, stride=4), :] = value
         if turn == 0:
             own_data.start()
+            pl.semaphore_wait(barrier, devices - 1)
+            each_other(lambda device: row_copy(device).start())
 
         def send(at, carry):
             data_copy(block * per_block + (me + at) % per_block).start()

time: 44.7 us -> 44.9 us (level)
  no operation moved by 1% of the time
where the time goes in v4:
time: 44.9 us; the launch traced here: 44.6 us
  Pallas kernels  39.3 us (88%)
  local copies, waits for them, and re-layouts  5.25 us (12%)
    pallas_call x1, Pallas kernels, shards(): pl.pallas_call(functools.partial(whole_kernel, x_size, y_size), out_shape...  39.3 us
    unnamed x11, local copies, waits for them, and re-layouts  3.94 us

profile of v4, /device:TPU:1, one launch (start us, length us, event | category | flops | bytes accessed | tf_op | source)
XLA Modules:
  0.0 44.6 jit_solution(13609711994967264522)
XLA Ops:
  0.0 0.0 copy-start
  0.0 0.9 %slice_reduce_fusion.2 = (s32[2048]{0:T(1024)S(1)}, s32[2048]{0:T(1024)S(1)}, s32[2048]{0:T(1024)S(1)}) fusion(s32[3,1,1,2048]{3,2,1,0:T(1,128)} %param.9, s32[3,1,1,2048]{3,2,1,0:T(1,128)} %param.8), kind=kLoop, calls=%fused_computation.3 | loop fusion | bytes 49152 | tf_op jit(solution)/shard_map/slice | solution.py:269
  0.9 0.1 stack.9
  1.0 0.1 stack.11
  1.0 0.1 stack.10
  1.1 0.1 copy.12
  1.3 0.1 copy.13
  1.4 0.0 copy-start.3
  1.4 0.0 copy-start.4
  1.4 0.0 copy-done
  1.4 0.7 %copy-done.3 = s32[3,1,1,2048]{3,2,1,0:T(1,128)S(1)} copy-done((s32[3,1,1,2048]{3,2,1,0:T(1,128)S(1)}, s32[3,1,1,2048]{3,2,1,0:T(1,128)}, u32[]{:S(2)}) %copy-start.3) | copy-done | bytes 24600
  2.1 0.0 copy-done.4
  2.1 0.0 copy-start.1
  2.1 1.2 %copy-done.1 = f32[64,4096]{1,0:T(8,128)S(1)} copy-done((f32[64,4096]{1,0:T(8,128)S(1)}, f32[64,4096]{1,0:T(8,128)}, u32[]{:S(2)}) %copy-start.1) | copy-done | bytes 1048600
  3.3 0.0 copy-start.2
  3.3 1.0 %copy-done.2 = f32[4,4,64,64]{3,2,1,0:T(8,128)S(1)} copy-done((f32[4,4,64,64]{3,2,1,0:T(8,128)S(1)}, f32[4,4,64,64]{3,2,1,0:T(8,128)}, u32[]{:S(2)}) %copy-start.2) | copy-done | bytes 262168
  4.4 39.3 %shard_map.55 = f32[2048,128]{1,0:T(8,128)S(1)} custom-call(f32[2048,128]{1,0:T(8,128)S(1)} %bitcast.16, f32[4,4,64,64]{3,2,1,0:T(8,128)S(1)} %copy-done.2, f32[64,4096]{1,0:T(8,128)S(1)} %copy-done.1, s32[48,1,128]{2,1,0:T(1,128)S(1)} %bitcast.18, s32[48,1,128]{2,1,0:T(1,128)S(1)} %bitcast.17, s32[32,1,256]{2,1,0:T(1,128)S(1)} %reshape.36.blocks_ref), custom_call_target="tpu_custom_call" | custom-call | tf_op jit(solution)/shard_map/pallas_call | solution.py:280
  43.6 1.0 %copy.16 = f32[2,64,1,2,1024]{4,3,2,1,0:T(2,128)} copy(f32[2,64,1,2,1024]{4,3,2,1,0:T(2,128)S(1)} %bitcast.15) | data formatting | bytes 2097152
  (3 shorter events, 0.1 us)
Async XLA Ops:
  0.0 1.4 %copy-start = (f32[2,64,2,2,512]{4,3,2,1,0:T(2,128)S(1)}, f32[2,64,2,2,512]{4,3,2,1,0:T(2,128)}, u32[]{:S(2)}) copy-start(f32[2,64,2,2,512]{4,3,2,1,0:T(2,128)} %param.5) | copy-start | bytes 3145732
  1.4 0.7 %copy-start.3 = (s32[3,1,1,2048]{3,2,1,0:T(1,128)S(1)}, s32[3,1,1,2048]{3,2,1,0:T(1,128)}, u32[]{:S(2)}) copy-start(s32[3,1,1,2048]{3,2,1,0:T(1,128)} %param.9) | copy-start | bytes 73732
  1.4 0.7 %copy-start.4 = (s32[3,1,1,2048]{3,2,1,0:T(1,128)S(1)}, s32[3,1,1,2048]{3,2,1,0:T(1,128)}, u32[]{:S(2)}) copy-start(s32[3,1,1,2048]{3,2,1,0:T(1,128)} %param.8) | copy-start | bytes 73732
  2.1 1.2 %copy-start.1 = (f32[64,4096]{1,0:T(8,128)S(1)}, f32[64,4096]{1,0:T(8,128)}, u32[]{:S(2)}) copy-start(f32[64,4096]{1,0:T(8,128)} %travel_ref.1) | copy-start | bytes 3145732
  3.3 1.0 %copy-start.2 = (f32[4,4,64,64]{3,2,1,0:T(8,128)S(1)}, f32[4,4,64,64]{3,2,1,0:T(8,128)}, u32[]{:S(2)}) copy-start(f32[4,4,64,64]{3,2,1,0:T(8,128)} %interp_ref.1) | copy-start | bytes 786436
